TPU v7x, 512 devices: a whole 4x8x8 slice. The times are simulated.
512 devices in a mesh: expert: 8 (over x, core), tensor: 64 (over y, z).
Axes of the slice: x: 4, y: 8, z: 8, core: 2. Of those that a mesh axis runs over, the one named last changes fastest.
Arguments:
- tokens: bfloat16 [1536, 6144], P('tensor'), may hold values from -6 to 6
- expert_ids: int32 [1536, 2], P('tensor'), may hold values from 0 to 7, all different within a row; in each aligned block of 24 rows (0 to 23, 24 to 47, ...) at most 12 rows name the same one
- gate_units: int32 [1536, 2], P('tensor'), may hold values from 1 to 65535
- gate_weight: bfloat16 [8, 6144, 8192], P('expert', None, 'tensor'), may hold values from -0.078125 to 0.078125
- up_weight: bfloat16 [8, 6144, 8192], P('expert', None, 'tensor'), may hold values from -0.078125 to 0.078125
- down_weight: bfloat16 [8, 6144, 8192], P('expert', 'tensor'), may hold values from -0.0625 to 0.0625
Outputs:
- expert_mix: bfloat16 [1536, 6144], P('tensor', 'expert')
Inputs may be any that keep to these rules, and one draw needn't show every extreme that they name: `expert_ids`: within each aligned block of 24 rows (the tokens of one tensor index) the two ids of a row differ and no expert is named by more than 12 rows; in every draw some expert is named by exactly 12 rows of some block, and every expert is named somewhere.
All inputs are finite; a program needn't handle non-finite values.
Results may differ from a plain program's by a relative error of at most 0.0057.
Values may be sent and summed in bfloat16 or wider, within the bound.
A program may use at most 128 MiB of HBM per device.

v0:
```python
import jax
import jax.numpy as jnp
from jax import lax
from jax.sharding import PartitionSpec as P


def slot_tables(expert_ids, gate_units, expert_id, capacity):
    tok_rows = expert_ids.shape[0]
    top_count = expert_ids.shape[1]
    flat_route = expert_ids.reshape(-1)
    matches = (flat_route == expert_id).astype(jnp.int32)
    slot_rank = jnp.cumsum(matches) - matches
    slot_ids = jnp.arange(capacity, dtype=jnp.int32)
    assignment = jnp.where(
        (slot_rank[None, :] == slot_ids[:, None]) & (matches[None, :] == 1), 1.0, 0.0
    ).astype(jnp.float32)
    positions = jnp.arange(tok_rows * top_count, dtype=jnp.int32) // top_count
    owners = (positions[:, None] == jnp.arange(tok_rows, dtype=jnp.int32)[None, :]).astype(
        jnp.float32
    )
    unit_vals = gate_units.astype(jnp.float32)
    shares = unit_vals / jnp.sum(unit_vals, axis=1, keepdims=True)
    picker = jnp.dot(
        assignment, owners, precision=lax.Precision.HIGHEST, preferred_element_type=jnp.float32
    )
    weighted = jnp.dot(
        assignment,
        owners * shares.reshape(-1)[:, None],
        precision=lax.Precision.HIGHEST,
        preferred_element_type=jnp.float32,
    )
    return (picker, weighted)


def local(tokens, expert_ids, gate_units, gate_weight, up_weight, down_weight):
    experts = lax.axis_size("expert")
    expert_id = lax.axis_index("expert")
    tok_rows = tokens.shape[0]
    capacity = min(tok_rows, 4 * tok_rows // experts)
    picker, weighted = slot_tables(expert_ids, gate_units, expert_id, capacity)
    picked = jnp.dot(
        picker.astype(jnp.bfloat16), tokens, preferred_element_type=jnp.float32
    ).astype(jnp.bfloat16)
    w_gate = gate_weight[0]
    w_up = up_weight[0]
    w_down = down_weight[0]
    shard_piece = lax.all_gather(picked, "tensor", axis=0, tiled=True)
    gate_vals = jnp.dot(shard_piece, w_gate, preferred_element_type=jnp.float32)
    up_vals = jnp.dot(shard_piece, w_up, preferred_element_type=jnp.float32)
    hidden = (jax.nn.silu(gate_vals) * up_vals).astype(jnp.bfloat16)
    gathered = lax.all_gather(hidden, "tensor", axis=1, tiled=True)
    projected = lax.dot_general(
        gathered, w_down, (((1,), (1,)), ((), ())), preferred_element_type=jnp.float32
    )
    outputs = projected.astype(jnp.bfloat16)
    returned = lax.all_to_all(outputs, "tensor", split_axis=0, concat_axis=1, tiled=True)
    contribution = lax.dot_general(
        weighted,
        returned.astype(jnp.float32),
        (((0,), (0,)), ((), ())),
        precision=lax.Precision.HIGHEST,
        preferred_element_type=jnp.float32,
    )
    summed_all = lax.psum(contribution, "expert")
    col_width = contribution.shape[1] // experts
    mixed = lax.dynamic_slice_in_dim(summed_all, expert_id * col_width, col_width, 1)
    return mixed.astype(jnp.bfloat16)


def solution(mesh):
    return jax.shard_map(
        local,
        mesh=mesh,
        in_specs=(
            P("tensor", None),
            P("tensor", None),
            P("tensor", None),
            P("expert", None, "tensor"),
            P("expert", None, "tensor"),
            P("expert", "tensor", None),
        ),
        out_specs=P("tensor", "expert"),
        check_vma=False,
    )
```

profile of v0, /device:TPU:8, one launch (start us, length us, event | category | flops | bytes accessed | tf_op | source)
XLA Modules:
  0.0 349.5 jit_solution(7697855502720402069)
XLA Ops:
  6.5 0.0 copy-start
  6.5 0.8 compare_convert_fusion
  7.3 0.1 copy.17
  7.4 0.1 reshape.76
  7.5 0.1 reshape.79
  7.6 0.1 reduce-window.8
  7.7 0.1 reduce
  7.8 0.2 convolution_convert_fusion.1
  8.0 1.8 fusion
  9.9 0.0 all-gather.6.cloned.1.call-update
  9.9 0.0 all-gather.4.cloned.1.call-start
  9.9 124.4 %all-gather.6.cloned.1.call-done = bf16[64,12,6144]{2,1,0:T(8,128)(2,1)} async-done(((bf16[1,12,6144]{2,1,0:T(8,128)(2,1)}), bf16[64,12,6144]{2,1,0:T(8,128)(2,1)}) %all-gather.6.cloned.1.call-update) | async-done | bytes 9437200 | tf_op jit(solution)/shard_map/all_gather | solution.py:47
  134.3 13.7 %reshape.78 = bf16[768,6144]{1,0:T(8,128)(2,1)} reshape(bf16[64,12,6144]{2,1,0:T(8,128)(2,1)} %all-gather.6.cloned.1.call-done) | data formatting | bytes 18874368
  148.1 6.1 %fusion.5 = f32[768,128]{1,0:T(8,128)S(1)} fusion(bf16[768,6144]{1,0:T(8,128)(2,1)} %reshape.78, bf16[1,6144,128]{2,1,0:T(8,128)(2,1)S(1)} %copy-done), kind=kOutput, calls=%fused_computation.6 | convolution fusion | flops 1207959552 | bytes 11403264 | tf_op jit(solution)/shard_map/dot_general | solution.py:48
  154.2 0.3 copy-done.1
  154.5 0.4 copy-done.4
  155.0 3.3 fusion.10
  158.2 0.0 all-gather.4.cloned.1.call-update
  158.3 124.2 %all-gather.4.cloned.1.call-done = bf16[768,8192]{1,0:T(8,128)(2,1)} async-done(((bf16[768,128]{1,0:T(8,128)(2,1)}), bf16[768,8192]{1,0:T(8,128)(2,1)}) %all-gather.4.cloned.1.call-update) | async-done | bytes 12582928 | tf_op jit(solution)/shard_map/all_gather | solution.py:51
  282.5 8.6 %fusion.13 = bf16[768,96]{0,1:T(8,128)(2,1)S(1)} fusion(bf16[768,8192]{1,0:T(8,128)(2,1)} %all-gather.4.cloned.1.call-done, bf16[1,96,8192]{2,1,0:T(8,128)(2,1)S(1)} %copy-done.2), kind=kOutput, calls=%fused_computation.10 | convolution fusion | flops 1208033280 | bytes 14303232 | tf_op jit(solution)/shard_map/dot_general | solution.py:52
  291.1 0.2 copy.21
  291.3 0.8 all_to_all.14
  292.0 7.8 %all-to-all-start = ((bf16[64,12,96]{2,1,0:T(8,128)(2,1)}), bf16[64,12,96]{2,1,0:T(8,128)(2,1)S(1)}, u32[]{:S(2)}, u32[]{:S(2)}) async-start(bf16[64,12,96]{2,1,0:T(8,128)(2,1)} %all_to_all.14), calls=%async_computation | async-start | bytes 524288 | tf_op jit(solution)/shard_map/all_to_all | solution.py:56
  299.8 0.1 copy.20
  299.9 0.1 mul.20
  300.0 0.2 fusion.16
  300.2 12.0 %all-to-all-done = bf16[64,12,96]{2,1,0:T(8,128)(2,1)S(1)} async-done(((bf16[64,12,96]{2,1,0:T(8,128)(2,1)}), bf16[64,12,96]{2,1,0:T(8,128)(2,1)S(1)}, u32[]{:S(2)}, u32[]{:S(2)}) %all-to-all-start) | async-done | bytes 147488 | tf_op jit(solution)/shard_map/all_to_all | solution.py:56
  312.2 0.1 copy.22
  312.2 0.3 all_to_all.17
  312.5 0.4 fusion.39
  313.0 29.1 %all-reduce.1 = bf16[24,6144]{1,0:T(8,128)(2,1)S(1)} all-reduce(f32[24,6144]{1,0:T(8,128)S(1)} %fusion.39), channel_id=1, replica_groups=mesh['expert'=8,'tensor'=64] {'expert'}, use_global_device_ids=true, to_apply=%region_2.3 | all-reduce | flops 147456 | bytes 884736 | tf_op jit(solution)/shard_map/psum | solution.py:64
  342.0 0.6 dynamic-slice_convert_fusion
  (13 shorter events, 0.1 us)
Async XLA Ops:
  6.5 141.6 %copy-start = (bf16[1,6144,128]{2,1,0:T(8,128)(2,1)S(1)}, bf16[1,6144,128]{2,1,0:T(8,128)(2,1)}, u32[]{:S(2)}) copy-start(bf16[1,6144,128]{2,1,0:T(8,128)(2,1)} %param.9) | copy-start | bytes 4718596
  6.5 127.8 %all-gather.6.cloned.1.call-start = ((), (), s32[]{:S(2)}) async-start(), calls=%async_computation.2 | async-start | bytes 12779520 | tf_op jit(solution)/shard_map/all_gather | solution.py:47
  9.9 272.6 %all-gather.4.cloned.1.call-start = ((), (), s32[]{:S(2)}) async-start(), calls=%async_computation.1 | async-start | bytes 12779520 | tf_op jit(solution)/shard_map/all_gather | solution.py:51
  148.1 6.4 %copy-start.1 = (bf16[768,6144]{1,0:T(8,128)(2,1)S(1)}, bf16[768,6144]{1,0:T(8,128)(2,1)}, u32[]{:S(2)}) copy-start(bf16[768,6144]{1,0:T(8,128)(2,1)} %reshape.78) | copy-start | bytes 28311556
  148.1 6.9 %copy-start.4 = (bf16[1,6144,128]{2,1,0:T(8,128)(2,1)S(1)}, bf16[1,6144,128]{2,1,0:T(8,128)(2,1)}, u32[]{:S(2)}) copy-start(bf16[1,6144,128]{2,1,0:T(8,128)(2,1)} %param.10) | copy-start | bytes 4718596
  154.9 3.3 copy-start.3
  154.9 127.6 %copy-start.2 = (bf16[1,96,8192]{2,1,0:T(8,128)(2,1)S(1)}, bf16[1,96,8192]{2,1,0:T(8,128)(2,1)}, u32[]{:S(2)}) copy-start(bf16[1,96,8192]{2,1,0:T(8,128)(2,1)} %param.11) | copy-start | bytes 4718596
  292.0 20.1 %all-to-all-start = ((bf16[64,12,96]{2,1,0:T(8,128)(2,1)}), bf16[64,12,96]{2,1,0:T(8,128)(2,1)S(1)}, u32[]{:S(2)}, u32[]{:S(2)}) async-start(bf16[64,12,96]{2,1,0:T(8,128)(2,1)} %all_to_all.14), calls=%async_computation | async-start | bytes 524288 | tf_op jit(solution)/shard_map/all_to_all | solution.py:56
Sparse Core Ops, SparseCore 0:
  10.4 123.9 all-gather.5
  158.4 124.1 all-gather.3
where the time goes:
time: 350 us
  waiting for transfers between devices  261 us (75%)
  blocking collectives  29.1 us (8%)
  matrix products  20.7 us (6%)
  local copies, waits for them, and re-layouts  16.8 us (5%)
  between operations  13.5 us (4%)
  starting transfers between devices  7.81 us (2%)
    all_gather x1, waiting for transfers between devices, local(): shard_piece = lax.all_gather(picked, 'tensor', axis=0, tiled=True)  124 us
    all_gather x1, waiting for transfers between devices, local(): gathered = lax.all_gather(hidden, 'tensor', axis=1, tiled=True)  124 us
    psum x1, blocking collectives, local(): summed_all = lax.psum(contribution, 'expert')  29.1 us
    unnamed x11, local copies, waits for them, and re-layouts  14.5 us
    all_to_all x1, waiting for transfers between devices, local(): lax.all_to_all(outputs, 'tensor', split_axis=0, concat_axis=1, tiled=True)  12 us
    dot_general x1, matrix products, local(): lax.dot_general(gathered, w_down, (((1,), (1,)), ((), ())), preferred_ele...  8.57 us
    all_to_all x1, starting transfers between devices, local(): lax.all_to_all(outputs, 'tensor', split_axis=0, concat_axis=1, tiled=True)  7.77 us
  transfers between devices with their start and end apart: 3, of which 3 were waited for; matrix products, arithmetic and copies ran while one was open for 0% of the time, Pallas kernels for 0%

commit v1 on v0

--- a/solution.py
+++ b/solution.py
@@ -61,7 +61,11 @@
         precision=lax.Precision.HIGHEST,
         preferred_element_type=jnp.float32,
     )
-    summed_all = lax.psum(contribution, "expert")
+    summed_all = contribution
+    for hop in (1, 2, 4):
+        summed_all = summed_all + lax.ppermute(
+            summed_all, "expert", [(dev, dev ^ hop) for dev in range(8)]
+        )
     col_width = contribution.shape[1] // experts
     mixed = lax.dynamic_slice_in_dim(summed_all, expert_id * col_width, col_width, 1)
     return mixed.astype(jnp.bfloat16)

time: 350 us -> 362 us (1.034)
  the two profiles are of different devices: /device:TPU:8 before, /device:TPU:2 now
where the time goes in v1:
time: 362 us; the launch traced here: 361 us
  waiting for transfers between devices  293 us (81%)
  matrix products  20.6 us (6%)
  local copies, waits for them, and re-layouts  16.2 us (4%)
  starting transfers between devices  15.9 us (4%)
  between operations  13.5 us (4%)
    all_gather x1, waiting for transfers between devices, local(): shard_piece = lax.all_gather(picked, 'tensor', axis=0, tiled=True)  124 us
    all_gather x1, waiting for transfers between devices, local(): gathered = lax.all_gather(hidden, 'tensor', axis=1, tiled=True)  124 us
    ppermute x3, waiting for transfers between devices, local(): lax.ppermute(summed_all, 'expert', [(dev, dev ^ hop) for dev in range(8)])  30.9 us
    unnamed x11, local copies, waits for them, and re-layouts  14.5 us
    all_to_all x1, waiting for transfers between devices, local(): lax.all_to_all(outputs, 'tensor', split_axis=0, concat_axis=1, tiled=True)  13.3 us
    dot_general x1, matrix products, local(): lax.dot_general(gathered, w_down, (((1,), (1,)), ((), ())), preferred_ele...  8.57 us
    ppermute x3, starting transfers between devices, local(): lax.ppermute(summed_all, 'expert', [(dev, dev ^ hop) for dev in range(8)])  8.18 us
    all_to_all x1, starting transfers between devices, local(): lax.all_to_all(outputs, 'tensor', split_axis=0, concat_axis=1, tiled=True)  7.64 us
  transfers between devices with their start and end apart: 6, of which 6 were waited for; matrix products, arithmetic and copies ran while one was open for 0% of the time, Pallas kernels for 0%

profile of v1, /device:TPU:2, one launch (start us, length us, event | category | flops | bytes accessed | tf_op | source)
XLA Modules:
  0.0 360.9 jit_solution(2555757021935219371)
XLA Ops:
  6.5 0.8 compare_convert_fusion
  7.3 0.1 copy.17
  7.4 0.1 reshape.76
  7.5 0.1 reshape.79
  7.6 0.1 reduce-window.8
  7.7 0.1 reduce
  7.8 0.2 convolution_convert_fusion.1
  8.0 1.8 fusion
  9.9 124.5 %all-gather.6.cloned.1.call-done = bf16[64,12,6144]{2,1,0:T(8,128)(2,1)} async-done(((bf16[1,12,6144]{2,1,0:T(8,128)(2,1)}), bf16[64,12,6144]{2,1,0:T(8,128)(2,1)}) %all-gather.6.cloned.1.call-update) | async-done | bytes 9437200 | tf_op jit(solution)/shard_map/all_gather | solution.py:47
  134.4 13.7 %reshape.78 = bf16[768,6144]{1,0:T(8,128)(2,1)} reshape(bf16[64,12,6144]{2,1,0:T(8,128)(2,1)} %all-gather.6.cloned.1.call-done) | data formatting | bytes 18874368
  148.2 6.1 %fusion.5 = f32[768,128]{1,0:T(8,128)S(1)} fusion(bf16[768,6144]{1,0:T(8,128)(2,1)} %reshape.78, bf16[1,6144,128]{2,1,0:T(8,128)(2,1)S(1)} %copy-done), kind=kOutput, calls=%fused_computation.6 | convolution fusion | flops 1207959552 | bytes 11403264 | tf_op jit(solution)/shard_map/dot_general | solution.py:48
  154.3 0.3 copy-done.1
  154.6 0.4 copy-done.4
  155.0 3.3 fusion.10
  158.3 124.3 %all-gather.4.cloned.1.call-done = bf16[768,8192]{1,0:T(8,128)(2,1)} async-done(((bf16[768,128]{1,0:T(8,128)(2,1)}), bf16[768,8192]{1,0:T(8,128)(2,1)}) %all-gather.4.cloned.1.call-update) | async-done | bytes 12582928 | tf_op jit(solution)/shard_map/all_gather | solution.py:51
  282.6 8.6 %fusion.13 = bf16[768,96]{0,1:T(8,128)(2,1)S(1)} fusion(bf16[768,8192]{1,0:T(8,128)(2,1)} %all-gather.4.cloned.1.call-done, bf16[1,96,8192]{2,1,0:T(8,128)(2,1)S(1)} %copy-done.2), kind=kOutput, calls=%fused_computation.10 | convolution fusion | flops 1208033280 | bytes 14303232 | tf_op jit(solution)/shard_map/dot_general | solution.py:52
  291.2 0.2 copy.21
  291.4 0.8 all_to_all.14
  292.1 7.6 %all-to-all-start = ((bf16[64,12,96]{2,1,0:T(8,128)(2,1)}), bf16[64,12,96]{2,1,0:T(8,128)(2,1)S(1)}, u32[]{:S(2)}, u32[]{:S(2)}) async-start(bf16[64,12,96]{2,1,0:T(8,128)(2,1)} %all_to_all.14), calls=%async_computation | async-start | bytes 524288 | tf_op jit(solution)/shard_map/all_to_all | solution.py:56
  299.8 0.1 copy.20
  299.9 0.1 mul.20
  300.0 0.2 fusion.17
  300.2 13.3 %all-to-all-done = bf16[64,12,96]{2,1,0:T(8,128)(2,1)S(1)} async-done(((bf16[64,12,96]{2,1,0:T(8,128)(2,1)}), bf16[64,12,96]{2,1,0:T(8,128)(2,1)S(1)}, u32[]{:S(2)}, u32[]{:S(2)}) %all-to-all-start) | async-done | bytes 147488 | tf_op jit(solution)/shard_map/all_to_all | solution.py:56
  313.5 0.3 all_to_all.17
  313.8 0.4 fusion.40
  314.3 1.9 collective-permute-start
  316.2 2.0 collective-permute-done
  318.2 2.4 collective-permute-start.1
  320.6 14.9 %collective-permute-done.1 = f32[24,6144]{1,0:T(8,128)S(1)} collective-permute-done((f32[24,6144]{1,0:T(8,128)S(1)}, f32[24,6144]{1,0:T(8,128)S(1)}, u32[]{:S(2)}, u32[]{:S(2)}) %collective-permute-start.1) | collective-permute-done | bytes 589856 | tf_op jit(solution)/shard_map/ppermute | solution.py:66
  335.5 3.9 %collective-permute-start.2 = (f32[24,6144]{1,0:T(8,128)S(1)}, f32[24,6144]{1,0:T(8,128)S(1)}, u32[]{:S(2)}, u32[]{:S(2)}) collective-permute-start(f32[24,6144]{1,0:T(8,128)S(1)} %add.23), channel_id=1, source_target_pairs={{0,256},{64,320},{128,384},{192,448},{256,0},{320,64},{384,128},{4... | collective-permute-start | bytes 1769480 | tf_op jit(solution)/shard_map/ppermute | solution.py:66
  339.4 14.0 %collective-permute-done.2 = f32[24,6144]{1,0:T(8,128)S(1)} collective-permute-done((f32[24,6144]{1,0:T(8,128)S(1)}, f32[24,6144]{1,0:T(8,128)S(1)}, u32[]{:S(2)}, u32[]{:S(2)}) %collective-permute-start.2) | collective-permute-done | bytes 589856 | tf_op jit(solution)/shard_map/ppermute | solution.py:66
  353.5 0.6 fusion.16
  (20 shorter events, 0.3 us)
Async XLA Ops:
  6.5 141.6 %copy-start = (bf16[1,6144,128]{2,1,0:T(8,128)(2,1)S(1)}, bf16[1,6144,128]{2,1,0:T(8,128)(2,1)}, u32[]{:S(2)}) copy-start(bf16[1,6144,128]{2,1,0:T(8,128)(2,1)} %param.9) | copy-start | bytes 4718596
  6.5 127.9 %all-gather.6.cloned.1.call-start = ((), (), s32[]{:S(2)}) async-start(), calls=%async_computation.2 | async-start | bytes 12779520 | tf_op jit(solution)/shard_map/all_gather | solution.py:47
  9.9 272.7 %all-gather.4.cloned.1.call-start = ((), (), s32[]{:S(2)}) async-start(), calls=%async_computation.1 | async-start | bytes 12779520 | tf_op jit(solution)/shard_map/all_gather | solution.py:51
  148.2 6.4 %copy-start.1 = (bf16[768,6144]{1,0:T(8,128)(2,1)S(1)}, bf16[768,6144]{1,0:T(8,128)(2,1)}, u32[]{:S(2)}) copy-start(bf16[768,6144]{1,0:T(8,128)(2,1)} %reshape.78) | copy-start | bytes 28311556
  148.2 6.9 %copy-start.4 = (bf16[1,6144,128]{2,1,0:T(8,128)(2,1)S(1)}, bf16[1,6144,128]{2,1,0:T(8,128)(2,1)}, u32[]{:S(2)}) copy-start(bf16[1,6144,128]{2,1,0:T(8,128)(2,1)} %param.10) | copy-start | bytes 4718596
  155.0 3.3 copy-start.3
  155.0 127.6 %copy-start.2 = (bf16[1,96,8192]{2,1,0:T(8,128)(2,1)S(1)}, bf16[1,96,8192]{2,1,0:T(8,128)(2,1)}, u32[]{:S(2)}) copy-start(bf16[1,96,8192]{2,1,0:T(8,128)(2,1)} %param.11) | copy-start | bytes 4718596
  292.1 21.3 %all-to-all-start = ((bf16[64,12,96]{2,1,0:T(8,128)(2,1)}), bf16[64,12,96]{2,1,0:T(8,128)(2,1)S(1)}, u32[]{:S(2)}, u32[]{:S(2)}) async-start(bf16[64,12,96]{2,1,0:T(8,128)(2,1)} %all_to_all.14), calls=%async_computation | async-start | bytes 524288 | tf_op jit(solution)/shard_map/all_to_all | solution.py:56
  314.3 3.9 %collective-permute-start = (f32[24,6144]{1,0:T(8,128)S(1)}, f32[24,6144]{1,0:T(8,128)S(1)}, u32[]{:S(2)}, u32[]{:S(2)}) collective-permute-start(f32[24,6144]{1,0:T(8,128)S(1)} %fusion.40), channel_id=1, source_target_pairs={{0,64},{64,0},{128,192},{192,128},{256,320},{320,256},{384,448},{4... | collective-permute-start | bytes 1769480 | tf_op jit(solution)/shard_map/ppermute | solution.py:66
  318.2 17.3 %collective-permute-start.1 = (f32[24,6144]{1,0:T(8,128)S(1)}, f32[24,6144]{1,0:T(8,128)S(1)}, u32[]{:S(2)}, u32[]{:S(2)}) collective-permute-start(f32[24,6144]{1,0:T(8,128)S(1)} %add.22), channel_id=1, source_target_pairs={{0,128},{64,192},{128,0},{192,64},{256,384},{320,448},{384,256},{4... | collective-permute-start | bytes 1769480 | tf_op jit(solution)/shard_map/ppermute | solution.py:66
  335.5 17.9 %collective-permute-start.2 = (f32[24,6144]{1,0:T(8,128)S(1)}, f32[24,6144]{1,0:T(8,128)S(1)}, u32[]{:S(2)}, u32[]{:S(2)}) collective-permute-start(f32[24,6144]{1,0:T(8,128)S(1)} %add.23), channel_id=1, source_target_pairs={{0,256},{64,320},{128,384},{192,448},{256,0},{320,64},{384,128},{4... | collective-permute-start | bytes 1769480 | tf_op jit(solution)/shard_map/ppermute | solution.py:66
Sparse Core Ops, SparseCore 0:
  10.4 123.9 all-gather.5
  158.4 124.1 all-gather.3
